TPU v7x, 128 devices: a whole 4x4x4 slice. The times are simulated.
128 devices in a mesh: row: 16 (over x, y), col: 8 (over z, core).
Axes of the slice: x: 4, y: 4, z: 4, core: 2. Of those that a mesh axis runs over, the one named last changes fastest.
Arguments:
- features: bfloat16 [49152, 256], P(('row', 'col')), may hold values from -6 to 6
- weight: bfloat16 [256, 256], replicated, may hold values from -0.375 to 0.375
- out_bias: float32 [256], replicated, may hold values from -3 to 3
- cotangent: bfloat16 [49152, 256], P(('row', 'col')), may hold values from -6 to 6
- adj_tiles: bfloat16 [16, 8, 24, 16, 128, 128], P('row', 'col'), may hold values from -0.125 to 0.125
- tile_cols: int32 [16, 8, 24, 16], P('row', 'col'), may hold values from 0 to 47, as said below
- tile_counts: int32 [16, 8, 24], P('row', 'col'), may hold values from 1 to 16, as said below
Outputs:
- activated: bfloat16 [49152, 256], P(('row', 'col'))
- grad_features: bfloat16 [49152, 256], P(('row', 'col'))
- grad_weight: float32 [256, 256], replicated
- grad_bias: float32 [256], replicated
Inputs may be any that keep to these rules, and one draw needn't show every extreme that they name: `tile_cols`: within a tile row of a block the 16 column numbers are distinct. `tile_counts`: every block has a tile row whose 16 slots are all live.
All inputs are finite; a program needn't handle non-finite values.
Results may differ from a plain program's by a relative error of at most 0.02.
Values may be sent and summed in bfloat16 or wider, within the bound.
No kernel may reach another device: no remote copies, remote signals or barrier semaphores. Data moves between devices by JAX's collectives and lax.ppermute only.
A program may use at most 192 MiB of HBM per device.

v0:
```python
import jax
import jax.numpy as jnp
from jax import lax
from jax.sharding import PartitionSpec as P


def tile_products(blocks, columns, live_mask, panel_tiles):
    accumulated = jnp.zeros((blocks.shape[0], blocks.shape[2], panel_tiles.shape[2]), jnp.float32)
    for position in range(blocks.shape[1]):
        picked = jnp.take(panel_tiles, columns[:, position], axis=0)
        product = jnp.einsum(
            "tab,tbf->taf", blocks[:, position], picked, preferred_element_type=jnp.float32
        )
        accumulated = accumulated + product * live_mask[:, position, None, None]
    return accumulated


def shards(features, weight, out_bias, cotangent, adj_tiles, tile_cols, tile_counts):
    node_dev = features.shape[0]
    feat_width = features.shape[1]
    tile_size = adj_tiles.shape[-1]
    slot_count = adj_tiles.shape[3]
    tile_rows = adj_tiles.shape[2]
    row_count = lax.axis_size("row")
    col_count = lax.axis_size("col")
    column_tiles = row_count * node_dev // tile_size
    blocks = adj_tiles.reshape(tile_rows, slot_count, tile_size, tile_size)
    columns = tile_cols.reshape(tile_rows, slot_count)
    slot_iota = lax.broadcasted_iota(jnp.int32, (tile_rows, slot_count), 1)
    live_mask = (slot_iota < tile_counts.reshape(tile_rows, 1)).astype(jnp.float32)
    gathered = jnp.dot(
        lax.all_gather(features, "row", axis=0, tiled=True),
        weight,
        preferred_element_type=jnp.float32,
    ).astype(jnp.bfloat16)
    panel_tiles = gathered.reshape(column_tiles, tile_size, feat_width)
    accumulated = tile_products(blocks, columns, live_mask, panel_tiles)
    rounded = accumulated.astype(jnp.bfloat16).astype(jnp.float32)
    summed = lax.psum_scatter(
        rounded.reshape(tile_rows * tile_size, feat_width).astype(jnp.bfloat16),
        "col",
        scatter_dimension=0,
        tiled=True,
    ).astype(jnp.float32)
    preact = summed + out_bias
    sigmoid_val = jax.nn.sigmoid(preact)
    activated = (preact * sigmoid_val).astype(jnp.bfloat16)
    grad_preact = (
        cotangent.astype(jnp.float32) * sigmoid_val * (1.0 + preact * (1.0 - sigmoid_val))
    ).astype(jnp.bfloat16)
    initial = jnp.zeros((column_tiles, tile_size, feat_width), jnp.float32)
    running = initial
    shard_rows = lax.all_gather(grad_preact, "col", axis=0, tiled=True)
    row_tiles = shard_rows.shape[0] // tile_size
    grad_tiles = shard_rows.reshape(row_tiles, tile_size, feat_width)
    for position in range(slot_count):
        product = jnp.einsum(
            "tab,taf->tbf", blocks[:, position], grad_tiles, preferred_element_type=jnp.float32
        )
        running = running.at[columns[:, position]].add(product * live_mask[:, position, None, None])
    back_rounded = running.astype(jnp.bfloat16).astype(jnp.float32)
    grad_projected = lax.psum_scatter(
        back_rounded.reshape(column_tiles * tile_size, feat_width).astype(jnp.bfloat16),
        "row",
        scatter_dimension=0,
        tiled=True,
    )
    grad_features = lax.dot_general(
        grad_projected, weight, (((1,), (1,)), ((), ())), preferred_element_type=jnp.float32
    ).astype(jnp.bfloat16)
    weight_part = lax.dot_general(
        features, grad_projected, (((0,), (0,)), ((), ())), preferred_element_type=jnp.float32
    )
    bias_part = jnp.sum(grad_preact.astype(jnp.float32), axis=0)
    scale_factor = (node_dev * row_count * col_count) ** (-0.5)
    weight_total, bias_total = lax.psum((weight_part, bias_part), ("row", "col"))
    return (activated, grad_features, weight_total * scale_factor, bias_total * scale_factor)


def solution(mesh):
    in_specs = (
        P(("row", "col"), None),
        P(),
        P(),
        P(("row", "col"), None),
        P("row", "col", None, None, None, None),
        P("row", "col", None, None),
        P("row", "col", None),
    )
    out_specs = (P(("row", "col"), None), P(("row", "col"), None), P(), P())
    return jax.shard_map(shards, mesh=mesh, in_specs=in_specs, out_specs=out_specs, check_vma=False)
```

profile of v0, /device:TPU:1, one launch (start us, length us, event | category | flops | bytes accessed | tf_op | source)
XLA Modules:
  0.0 643.4 jit_solution(12031219204387796156)
XLA Ops:
  8.0 11.9 %copy.96 = bf16[1,1,24,16,128,128]{5,4,2,3,1,0:T(8,128)(2,1)} copy(bf16[1,1,24,16,128,128]{5,4,3,2,1,0:T(8,128)(2,1)} %param.13) | data formatting | bytes 25165824 | tf_op args[4]
  20.0 40.4 %all-gather.3.cloned.1.call-done = bf16[6144,256]{1,0:T(8,128)(2,1)} async-done(((bf16[384,256]{1,0:T(8,128)(2,1)}), bf16[6144,256]{1,0:T(8,128)(2,1)}) %all-gather.3.cloned.1.call-update) | async-done | bytes 3145744 | tf_op jit(solution)/shard_map/all_gather | solution.py:32
  133.4 17.8 %bitcast_convert_fusion = bf16[24,128,256]{2,1,0:T(8,128)(2,1)} fusion(f32[24,256,128]{1,2,0:T(8,128)} %fusion.1, f32[24,256,128]{1,2,0:T(8,128)} %fusion.3, f32[24,256,128]{1,2,0:T(8,128)} %fusion.5, f32[24,256,128]{1,2,0:T(8,128)} %fusion.7, f32[24,256,128]{1,2,0:T(8,128)} %fusion.9, f32[24,256,128]{1,2,0:T(8,128)S(1)} %fusion.11, ...), kind=kOutput, calls=%fused_computation.34 | convolution fusion | flops 227278848 | bytes 51119640 | tf_op jit(solution)/shard_map/tab,tbf->taf/dot_general | solution.py:11
  151.3 29.8 %reduce-scatter.3.cloned.1.call-done = bf16[384,256]{1,0:T(8,128)(2,1)} async-done(((bf16[3072,256]{1,0:T(8,128)(2,1)}), bf16[384,256]{1,0:T(8,128)(2,1)}) %reduce-scatter.3.cloned.1.call-update) | async-done | bytes 196624 | tf_op jit(solution)/shard_map/reduce_scatter | solution.py:39
  183.1 26.9 %all-gather.5.cloned.1.call-done = bf16[3072,256]{1,0:T(8,128)(2,1)} async-done(((bf16[384,256]{1,0:T(8,128)(2,1)}), bf16[3072,256]{1,0:T(8,128)(2,1)}) %all-gather.5.cloned.1.call-update) | async-done | bytes 1572880 | tf_op jit(solution)/shard_map/all_gather | solution.py:53
  256.1 10.0 %scatter_fusion = f32[48,128,256]{2,1,0:T(8,128)} fusion(f32[48,128,256]{2,1,0:T(8,128)} %broadcast_in_dim.11, s32[24]{0:T(128)S(1)} %get-tuple-element.49, f32[24,128,256]{2,1,0:T(8,128)} %multiply_bitcast_fusion.15), kind=kCustom, calls=%fused_computation.16 | custom fusion | flops 786432 | bytes 9437280 | tf_op jit(solution)/shard_map/scatter-add | solution.py:60
  266.1 9.3 %scatter_fusion.1 = f32[48,128,256]{2,1,0:T(8,128)} fusion(f32[48,128,256]{2,1,0:T(8,128)} %scatter_fusion, s32[24]{0:T(128)S(1)} %get-tuple-element.50, f32[24,128,256]{2,1,0:T(8,128)} %multiply_bitcast_fusion.14), kind=kCustom, calls=%fused_computation.17 | custom fusion | flops 786432 | bytes 9437280 | tf_op jit(solution)/shard_map/scatter-add | solution.py:60
  275.4 9.3 %scatter_fusion.2 = f32[48,128,256]{2,1,0:T(8,128)} fusion(f32[48,128,256]{2,1,0:T(8,128)} %scatter_fusion.1, s32[24]{0:T(128)S(1)} %get-tuple-element.51, f32[24,128,256]{2,1,0:T(8,128)} %multiply_bitcast_fusion.13), kind=kCustom, calls=%fused_computation.18 | custom fusion | flops 786432 | bytes 9437280 | tf_op jit(solution)/shard_map/scatter-add | solution.py:60
  284.7 9.4 %scatter_fusion.3 = f32[48,128,256]{2,1,0:T(8,128)} fusion(f32[48,128,256]{2,1,0:T(8,128)} %scatter_fusion.2, s32[24]{0:T(128)S(1)} %get-tuple-element.52, f32[24,128,256]{2,1,0:T(8,128)} %multiply_bitcast_fusion.12), kind=kCustom, calls=%fused_computation.19 | custom fusion | flops 786432 | bytes 9437280 | tf_op jit(solution)/shard_map/scatter-add | solution.py:60
  294.1 9.3 %scatter_fusion.4 = f32[48,128,256]{2,1,0:T(8,128)} fusion(f32[48,128,256]{2,1,0:T(8,128)} %scatter_fusion.3, s32[24]{0:T(128)S(1)} %get-tuple-element.53, f32[24,128,256]{2,1,0:T(8,128)} %multiply_bitcast_fusion.11), kind=kCustom, calls=%fused_computation.20 | custom fusion | flops 786432 | bytes 9437280 | tf_op jit(solution)/shard_map/scatter-add | solution.py:60
  303.4 9.4 %scatter_fusion.5 = f32[48,128,256]{2,1,0:T(8,128)} fusion(f32[48,128,256]{2,1,0:T(8,128)} %scatter_fusion.4, s32[24]{0:T(128)S(1)} %get-tuple-element.54, f32[24,128,256]{2,1,0:T(8,128)} %multiply_bitcast_fusion.10), kind=kCustom, calls=%fused_computation.21 | custom fusion | flops 786432 | bytes 9437280 | tf_op jit(solution)/shard_map/scatter-add | solution.py:60
  312.8 9.5 %scatter_fusion.6 = f32[48,128,256]{2,1,0:T(8,128)} fusion(f32[48,128,256]{2,1,0:T(8,128)} %scatter_fusion.5, s32[24]{0:T(128)S(1)} %get-tuple-element.55, f32[24,128,256]{2,1,0:T(8,128)} %multiply_bitcast_fusion.9), kind=kCustom, calls=%fused_computation.22 | custom fusion | flops 786432 | bytes 9437280 | tf_op jit(solution)/shard_map/scatter-add | solution.py:60
  322.3 9.4 %scatter_fusion.7 = f32[48,128,256]{2,1,0:T(8,128)} fusion(f32[48,128,256]{2,1,0:T(8,128)} %scatter_fusion.6, s32[24]{0:T(128)S(1)} %get-tuple-element.56, f32[24,128,256]{2,1,0:T(8,128)} %multiply_bitcast_fusion.8), kind=kCustom, calls=%fused_computation.23 | custom fusion | flops 786432 | bytes 9437280 | tf_op jit(solution)/shard_map/scatter-add | solution.py:60
  331.8 9.3 %scatter_fusion.8 = f32[48,128,256]{2,1,0:T(8,128)} fusion(f32[48,128,256]{2,1,0:T(8,128)} %scatter_fusion.7, s32[24]{0:T(128)S(1)} %get-tuple-element.57, f32[24,128,256]{2,1,0:T(8,128)} %multiply_bitcast_fusion.7), kind=kCustom, calls=%fused_computation.24 | custom fusion | flops 786432 | bytes 9437280 | tf_op jit(solution)/shard_map/scatter-add | solution.py:60
  341.1 9.6 %scatter_fusion.9 = f32[48,128,256]{2,1,0:T(8,128)} fusion(f32[48,128,256]{2,1,0:T(8,128)} %scatter_fusion.8, s32[24]{0:T(128)S(1)} %get-tuple-element.58, f32[24,128,256]{2,1,0:T(8,128)} %multiply_bitcast_fusion.6), kind=kCustom, calls=%fused_computation.25 | custom fusion | flops 786432 | bytes 9437280 | tf_op jit(solution)/shard_map/scatter-add | solution.py:60
  350.6 9.4 %scatter_fusion.10 = f32[48,128,256]{2,1,0:T(8,128)} fusion(f32[48,128,256]{2,1,0:T(8,128)} %scatter_fusion.9, s32[24]{0:T(128)S(1)} %get-tuple-element.59, f32[24,128,256]{2,1,0:T(8,128)} %multiply_bitcast_fusion.5), kind=kCustom, calls=%fused_computation.26 | custom fusion | flops 786432 | bytes 9437280 | tf_op jit(solution)/shard_map/scatter-add | solution.py:60
  360.0 9.4 %scatter_fusion.11 = f32[48,128,256]{2,1,0:T(8,128)} fusion(f32[48,128,256]{2,1,0:T(8,128)} %scatter_fusion.10, s32[24]{0:T(128)S(1)} %get-tuple-element.60, f32[24,128,256]{2,1,0:T(8,128)} %multiply_bitcast_fusion.4), kind=kCustom, calls=%fused_computation.27 | custom fusion | flops 786432 | bytes 9437280 | tf_op jit(solution)/shard_map/scatter-add | solution.py:60
  369.5 9.3 %scatter_fusion.12 = f32[48,128,256]{2,1,0:T(8,128)} fusion(f32[48,128,256]{2,1,0:T(8,128)} %scatter_fusion.11, s32[24]{0:T(128)S(1)} %get-tuple-element.61, f32[24,128,256]{2,1,0:T(8,128)} %multiply_bitcast_fusion.3), kind=kCustom, calls=%fused_computation.28 | custom fusion | flops 786432 | bytes 9437280 | tf_op jit(solution)/shard_map/scatter-add | solution.py:60
  378.8 9.5 %scatter_fusion.13 = f32[48,128,256]{2,1,0:T(8,128)} fusion(f32[48,128,256]{2,1,0:T(8,128)} %scatter_fusion.12, s32[24]{0:T(128)S(1)} %get-tuple-element.62, f32[24,128,256]{2,1,0:T(8,128)} %multiply_bitcast_fusion.2), kind=kCustom, calls=%fused_computation.29 | custom fusion | flops 786432 | bytes 9437280 | tf_op jit(solution)/shard_map/scatter-add | solution.py:60
  388.3 9.4 %scatter_fusion.14 = f32[48,128,256]{2,1,0:T(8,128)} fusion(f32[48,128,256]{2,1,0:T(8,128)} %scatter_fusion.13, s32[24]{0:T(128)S(1)} %get-tuple-element.63, f32[24,128,256]{2,1,0:T(8,128)} %multiply_bitcast_fusion.1), kind=kCustom, calls=%fused_computation.30 | custom fusion | flops 786432 | bytes 9437280 | tf_op jit(solution)/shard_map/scatter-add | solution.py:60
  397.7 8.4 %scatter_fusion.15 = f32[48,128,256]{2,1,0:T(8,128)} fusion(f32[48,128,256]{2,1,0:T(8,128)} %scatter_fusion.14, s32[24]{0:T(128)S(1)} %get-tuple-element.48, f32[24,128,256]{2,1,0:T(8,128)S(1)} %multiply_bitcast_fusion), kind=kCustom, calls=%fused_computation.31 | custom fusion | flops 786432 | bytes 9437280 | tf_op jit(solution)/shard_map/scatter-add | solution.py:60
  411.1 64.7 %psum.15 = f32[256]{0:T(256)S(1)} all-reduce(f32[256]{0:T(256)S(1)} %get-tuple-element.13), channel_id=1, replica_groups=mesh['row'=16,'col'=8] {'row','col'}, use_global_device_ids=true, to_apply=%region_20.22 | all-reduce | flops 256 | bytes 2048 | tf_op jit(solution)/shard_map/psum | solution.py:76
  476.4 9.1 %reduce-scatter.5.cloned.1.call-done = bf16[384,256]{1,0:T(8,128)(2,1)} async-done(((bf16[6144,256]{1,0:T(8,128)(2,1)}), bf16[384,256]{1,0:T(8,128)(2,1)}) %reduce-scatter.5.cloned.1.call-update) | async-done | bytes 196624 | tf_op jit(solution)/shard_map/reduce_scatter | solution.py:62
  489.3 145.6 %all-reduce.2.cloned.1.call-done = f32[256,256]{0,1:T(8,128)} async-done(((f32[256,256]{0,1:T(8,128)}), f32[256,256]{0,1:T(8,128)}) %all-reduce.2.cloned.1.call-update) | async-done | bytes 262160 | tf_op jit(solution)/shard_map/psum | solution.py:76
  (134 shorter events, 132.9 us)
Async XLA Ops:
  7.2 53.3 %copy-start = (bf16[256,256]{1,0:T(8,128)(2,1)S(1)}, bf16[256,256]{1,0:T(8,128)(2,1)}, u32[]{:S(2)}) copy-start(bf16[256,256]{1,0:T(8,128)(2,1)} %param.10) | copy-start | bytes 393220
  7.2 53.2 %all-gather.3.cloned.1.call-start = ((), (), s32[]{:S(2)}) async-start(), calls=%async_computation.2 | async-start | bytes 3342336 | tf_op jit(solution)/shard_map/all_gather | solution.py:32
  7.9 11.9 %copy-start.18 = (s32[1,1,24,16]{2,3,1,0:T(8,128)S(1)}, s32[1,1,24,16]{2,3,1,0:T(8,128)}, u32[]{:S(2)}) copy-start(s32[1,1,24,16]{2,3,1,0:T(8,128)} %param.14) | copy-start | bytes 4612
  7.9 12.1 %copy-start.20 = (s32[1,1,24]{2,1,0:T(1,128)S(1)}, s32[1,1,24]{2,1,0:T(1,128)}, u32[]{:S(2)}) copy-start(s32[1,1,24]{2,1,0:T(1,128)} %param.15) | copy-start | bytes 292
  7.9 173.2 %reduce-scatter.3.cloned.1.call-start = ((), (), s32[]{:S(2)}) async-start(), calls=%async_computation.3 | async-start | bytes 1769472 | tf_op jit(solution)/shard_map/reduce_scatter | solution.py:39
  93.1 2.5 copy-start.15
  93.1 16.8 %slice-start = ((s8[12582912]{0:T(1024)(128)(4,1)}), s8[4194304]{0:T(1024)(128)(4,1)S(1)}, s32[]{:S(2)}) async-start(s8[12582912]{0:T(1024)(128)(4,1)} %bitcast.286), calls=%async_computation.7 | async-start | bytes 8388608
  95.5 3.6 copy-start.13
  95.6 14.4 %slice-start.1 = ((s8[12582912]{0:T(1024)(128)(4,1)}), s8[4194304]{0:T(1024)(128)(4,1)S(1)}, s32[]{:S(2)}) async-start(s8[12582912]{0:T(1024)(128)(4,1)} %bitcast.286), calls=%async_computation.8 | async-start | bytes 8388608
  99.2 3.6 copy-start.14
  102.7 3.6 copy-start.11
  102.7 7.2 %slice-start.2 = ((s8[12582912]{0:T(1024)(128)(4,1)}), s8[4194304]{0:T(1024)(128)(4,1)S(1)}, s32[]{:S(2)}) async-start(s8[12582912]{0:T(1024)(128)(4,1)} %bitcast.286), calls=%async_computation.9 | async-start | bytes 8388608
  106.4 3.6 copy-start.12
  128.7 2.5 copy-start.2
  133.4 47.7 %copy-start.17 = (bf16[384,256]{1,0:T(8,128)(2,1)S(1)}, bf16[384,256]{1,0:T(8,128)(2,1)}, u32[]{:S(2)}) copy-start(bf16[384,256]{1,0:T(8,128)(2,1)} %param.12) | copy-start | bytes 589828
  133.4 47.7 %copy-start.19 = (f32[256]{0:T(256)S(1)}, f32[256]{0:T(256)}, u32[]{:S(2)}) copy-start(f32[256]{0:T(256)} %param.11) | copy-start | bytes 3076
  151.3 58.8 %all-gather.5.cloned.1.call-start = ((), (), s32[]{:S(2)}) async-start(), calls=%async_computation.4 | async-start | bytes 1769472 | tf_op jit(solution)/shard_map/all_gather | solution.py:53
  183.0 302.5 %reduce-scatter.5.cloned.1.call-start = ((), (), s32[]{:S(2)}) async-start(), calls=%async_computation.5 | async-start | bytes 3342336 | tf_op jit(solution)/shard_map/reduce_scatter | solution.py:62
  210.1 4.2 copy-start.1
  210.1 18.3 %slice-start.3 = ((s8[12582912]{0:T(1024)(128)(4,1)}), s8[4194304]{0:T(1024)(128)(4,1)S(1)}, s32[]{:S(2)}) async-start(s8[12582912]{0:T(1024)(128)(4,1)} %bitcast.298), calls=%async_computation.10 | async-start | bytes 8388608
  214.2 14.1 %slice-start.4 = ((s8[12582912]{0:T(1024)(128)(4,1)}), s8[4194304]{0:T(1024)(128)(4,1)S(1)}, s32[]{:S(2)}) async-start(s8[12582912]{0:T(1024)(128)(4,1)} %bitcast.298), calls=%async_computation.11 | async-start | bytes 8388608
  221.2 7.1 %slice-start.5 = ((s8[12582912]{0:T(1024)(128)(4,1)}), s8[4194304]{0:T(1024)(128)(4,1)S(1)}, s32[]{:S(2)}) async-start(s8[12582912]{0:T(1024)(128)(4,1)} %bitcast.298), calls=%async_computation.12 | async-start | bytes 8388608
  411.0 74.5 %copy-start.16 = (bf16[384,256]{1,0:T(8,128)(2,1)S(1)}, bf16[384,256]{1,0:T(8,128)(2,1)}, u32[]{:S(2)}) copy-start(bf16[384,256]{1,0:T(8,128)(2,1)} %param.9) | copy-start | bytes 589828
  411.1 223.8 %all-reduce.2.cloned.1.call-start = ((), (), s32[]{:S(2)}) async-start(), calls=%async_computation.6 | async-start | bytes 524288 | tf_op jit(solution)/shard_map/psum | solution.py:76
  (8 other events, 18.8 us)
Sparse Core Ops, SparseCore 0:
  10.2 50.2 all-gather.2
  151.4 29.7 reduce-scatter.2
  183.4 26.6 all-gather.4
  411.2 74.3 reduce-scatter.4
  490.7 144.1 all-reduce.1
where the time goes:
time: 653 us; the launch traced here: 643 us
  waiting for transfers between devices  253 us (39%)
  other arithmetic  158 us (24%)
  matrix products  107 us (16%)
  blocking collectives  64.7 us (10%)
  local copies, waits for them, and re-layouts  46 us (7%)
  between operations  14.2 us (2%)
    scatter-add x16, other arithmetic, shards(): running.at[columns[:, position]]  150 us
    psum x1, waiting for transfers between devices, shards(): lax.psum((weight_part, bias_part), ('row', 'col'))  146 us
    psum x1, blocking collectives, shards(): lax.psum((weight_part, bias_part), ('row', 'col'))  64.7 us
    dot_general x16, matrix products, tile_products(): jnp.einsum('tab,tbf->taf', blocks[:, position], picked, preferred_element...  58 us
    dot_general x16, matrix products, shards(): jnp.einsum('tab,taf->tbf', blocks[:, position], grad_tiles, preferred_ele...  42.6 us
    all_gather x1, waiting for transfers between devices, shards(): lax.all_gather(features, 'row', axis=0, tiled=True)  40.4 us
    reduce_scatter x1, waiting for transfers between devices, shards(): lax.psum_scatter(rounded.reshape(tile_rows * tile_size, feat_width).astyp...  29.8 us
    gather x16, local copies, waits for them, and re-layouts, tile_products(): picked = jnp.take(panel_tiles, columns[:, position], axis=0)  29.8 us
  transfers between devices with their start and end apart: 5, of which 5 were waited for; matrix products, arithmetic and copies ran while one was open for 2% of the time, Pallas kernels for 0%

commit v1 on v0

--- a/solution.py
+++ b/solution.py
@@ -2,6 +2,11 @@
 import jax.numpy as jnp
 from jax import lax
 from jax.sharding import PartitionSpec as P
+
+
+def by_each_axis(value, axis_one, axis_two):
+    inner = lax.psum(value, axis_one)
+    return lax.psum(inner, axis_two)
 
 
 def tile_products(blocks, columns, live_mask, panel_tiles):
@@ -73,7 +78,7 @@
     )
     bias_part = jnp.sum(grad_preact.astype(jnp.float32), axis=0)
     scale_factor = (node_dev * row_count * col_count) ** (-0.5)
-    weight_total, bias_total = lax.psum((weight_part, bias_part), ("row", "col"))
+    weight_total, bias_total = by_each_axis((weight_part, bias_part), "col", "row")
     return (activated, grad_features, weight_total * scale_factor, bias_total * scale_factor)
 
 

time: 653 us -> 655 us (level)
  blocking collectives: 64.7 us -> 45.4 us
  waiting for transfers between devices: 253 us -> 271 us
    reduce_scatter x1, waiting for transfers between devices: 9.14 us -> 74.2 us  [shards(): lax.psum_scatter(back_rounded.reshape(column_tiles * tile_size, feat_widt...]
    psum x1 -> x2, waiting for transfers between devices: 146 us -> 99.2 us  [the longest x1 84.4 us: by_each_axis(): return lax.psum(inner, axis_two)]
    psum x1 -> x2, blocking collectives: 64.7 us -> 45.4 us  [the longest x1 31.2 us: by_each_axis(): return lax.psum(inner, axis_two)]
  transfers between devices with their start and end apart: 5 -> 6, of which waited for: 5 -> 6; matrix products, arithmetic and copies ran while one was open for 2% -> 2% of each run, Pallas kernels for 0% -> 0%
where the time goes in v1:
time: 655 us; the launch traced here: 643 us
  waiting for transfers between devices  271 us (41%)
  other arithmetic  158 us (24%)
  matrix products  107 us (16%)
  local copies, waits for them, and re-layouts  46 us (7%)
  blocking collectives  45.4 us (7%)
  between operations  14.8 us (2%)
    scatter-add x16, other arithmetic, shards(): running.at[columns[:, position]]  150 us
    psum x1, waiting for transfers between devices, by_each_axis(): return lax.psum(inner, axis_two)  84.4 us
    reduce_scatter x1, waiting for transfers between devices, shards(): lax.psum_scatter(back_rounded.reshape(column_tiles * tile_size, feat_widt...  74.2 us
    dot_general x16, matrix products, tile_products(): jnp.einsum('tab,tbf->taf', blocks[:, position], picked, preferred_element...  58 us
    dot_general x16, matrix products, shards(): jnp.einsum('tab,taf->tbf', blocks[:, position], grad_tiles, preferred_ele...  42.6 us
    all_gather x1, waiting for transfers between devices, shards(): lax.all_gather(features, 'row', axis=0, tiled=True)  40.4 us
    psum x1, blocking collectives, by_each_axis(): return lax.psum(inner, axis_two)  31.2 us
    gather x16, local copies, waits for them, and re-layouts, tile_products(): picked = jnp.take(panel_tiles, columns[:, position], axis=0)  29.8 us
  transfers between devices with their start and end apart: 6, of which 6 were waited for; matrix products, arithmetic and copies ran while one was open for 2% of the time, Pallas kernels for 0%

profile of v1, /device:TPU:1, one launch (start us, length us, event | category | flops | bytes accessed | tf_op | source)
XLA Modules:
  0.0 643.4 jit_solution(12315616212110445543)
XLA Ops:
  8.0 11.9 %copy.96 = bf16[1,1,24,16,128,128]{5,4,2,3,1,0:T(8,128)(2,1)} copy(bf16[1,1,24,16,128,128]{5,4,3,2,1,0:T(8,128)(2,1)} %param.13) | data formatting | bytes 25165824 | tf_op args[4]
  20.0 40.4 %all-gather.3.cloned.1.call-done = bf16[6144,256]{1,0:T(8,128)(2,1)} async-done(((bf16[384,256]{1,0:T(8,128)(2,1)}), bf16[6144,256]{1,0:T(8,128)(2,1)}) %all-gather.3.cloned.1.call-update) | async-done | bytes 3145744 | tf_op jit(solution)/shard_map/all_gather | solution.py:37
  133.4 17.8 %bitcast_convert_fusion = bf16[24,128,256]{2,1,0:T(8,128)(2,1)} fusion(f32[24,256,128]{1,2,0:T(8,128)} %fusion.1, f32[24,256,128]{1,2,0:T(8,128)} %fusion.3, f32[24,256,128]{1,2,0:T(8,128)} %fusion.5, f32[24,256,128]{1,2,0:T(8,128)} %fusion.7, f32[24,256,128]{1,2,0:T(8,128)} %fusion.9, f32[24,256,128]{1,2,0:T(8,128)S(1)} %fusion.11, ...), kind=kOutput, calls=%fused_computation.34 | convolution fusion | flops 227278848 | bytes 51119640 | tf_op jit(solution)/shard_map/tab,tbf->taf/dot_general | solution.py:16
  151.3 29.8 %reduce-scatter.3.cloned.1.call-done = bf16[384,256]{1,0:T(8,128)(2,1)} async-done(((bf16[3072,256]{1,0:T(8,128)(2,1)}), bf16[384,256]{1,0:T(8,128)(2,1)}) %reduce-scatter.3.cloned.1.call-update) | async-done | bytes 196624 | tf_op jit(solution)/shard_map/reduce_scatter | solution.py:44
  183.0 27.0 %all-gather.5.cloned.1.call-done = bf16[3072,256]{1,0:T(8,128)(2,1)} async-done(((bf16[384,256]{1,0:T(8,128)(2,1)}), bf16[3072,256]{1,0:T(8,128)(2,1)}) %all-gather.5.cloned.1.call-update) | async-done | bytes 1572880 | tf_op jit(solution)/shard_map/all_gather | solution.py:58
  256.1 9.8 %scatter_fusion = f32[48,128,256]{2,1,0:T(8,128)} fusion(f32[48,128,256]{2,1,0:T(8,128)} %broadcast_in_dim.11, s32[24]{0:T(128)S(1)} %get-tuple-element.49, f32[24,128,256]{2,1,0:T(8,128)} %multiply_bitcast_fusion.15), kind=kCustom, calls=%fused_computation.16 | custom fusion | flops 786432 | bytes 9437280 | tf_op jit(solution)/shard_map/scatter-add | solution.py:65
  265.9 9.3 %scatter_fusion.1 = f32[48,128,256]{2,1,0:T(8,128)} fusion(f32[48,128,256]{2,1,0:T(8,128)} %scatter_fusion, s32[24]{0:T(128)S(1)} %get-tuple-element.50, f32[24,128,256]{2,1,0:T(8,128)} %multiply_bitcast_fusion.14), kind=kCustom, calls=%fused_computation.17 | custom fusion | flops 786432 | bytes 9437280 | tf_op jit(solution)/shard_map/scatter-add | solution.py:65
  284.5 9.4 %scatter_fusion.3 = f32[48,128,256]{2,1,0:T(8,128)} fusion(f32[48,128,256]{2,1,0:T(8,128)} %scatter_fusion.2, s32[24]{0:T(128)S(1)} %get-tuple-element.52, f32[24,128,256]{2,1,0:T(8,128)} %multiply_bitcast_fusion.12), kind=kCustom, calls=%fused_computation.19 | custom fusion | flops 786432 | bytes 9437280 | tf_op jit(solution)/shard_map/scatter-add | solution.py:65
  293.9 9.3 %scatter_fusion.4 = f32[48,128,256]{2,1,0:T(8,128)} fusion(f32[48,128,256]{2,1,0:T(8,128)} %scatter_fusion.3, s32[24]{0:T(128)S(1)} %get-tuple-element.53, f32[24,128,256]{2,1,0:T(8,128)} %multiply_bitcast_fusion.11), kind=kCustom, calls=%fused_computation.20 | custom fusion | flops 786432 | bytes 9437280 | tf_op jit(solution)/shard_map/scatter-add | solution.py:65
  303.2 9.4 %scatter_fusion.5 = f32[48,128,256]{2,1,0:T(8,128)} fusion(f32[48,128,256]{2,1,0:T(8,128)} %scatter_fusion.4, s32[24]{0:T(128)S(1)} %get-tuple-element.54, f32[24,128,256]{2,1,0:T(8,128)} %multiply_bitcast_fusion.10), kind=kCustom, calls=%fused_computation.21 | custom fusion | flops 786432 | bytes 9437280 | tf_op jit(solution)/shard_map/scatter-add | solution.py:65
  312.6 9.5 %scatter_fusion.6 = f32[48,128,256]{2,1,0:T(8,128)} fusion(f32[48,128,256]{2,1,0:T(8,128)} %scatter_fusion.5, s32[24]{0:T(128)S(1)} %get-tuple-element.55, f32[24,128,256]{2,1,0:T(8,128)} %multiply_bitcast_fusion.9), kind=kCustom, calls=%fused_computation.22 | custom fusion | flops 786432 | bytes 9437280 | tf_op jit(solution)/shard_map/scatter-add | solution.py:65
  322.1 9.4 %scatter_fusion.7 = f32[48,128,256]{2,1,0:T(8,128)} fusion(f32[48,128,256]{2,1,0:T(8,128)} %scatter_fusion.6, s32[24]{0:T(128)S(1)} %get-tuple-element.56, f32[24,128,256]{2,1,0:T(8,128)} %multiply_bitcast_fusion.8), kind=kCustom, calls=%fused_computation.23 | custom fusion | flops 786432 | bytes 9437280 | tf_op jit(solution)/shard_map/scatter-add | solution.py:65
  331.6 9.3 %scatter_fusion.8 = f32[48,128,256]{2,1,0:T(8,128)} fusion(f32[48,128,256]{2,1,0:T(8,128)} %scatter_fusion.7, s32[24]{0:T(128)S(1)} %get-tuple-element.57, f32[24,128,256]{2,1,0:T(8,128)} %multiply_bitcast_fusion.7), kind=kCustom, calls=%fused_computation.24 | custom fusion | flops 786432 | bytes 9437280 | tf_op jit(solution)/shard_map/scatter-add | solution.py:65
  340.9 9.6 %scatter_fusion.9 = f32[48,128,256]{2,1,0:T(8,128)} fusion(f32[48,128,256]{2,1,0:T(8,128)} %scatter_fusion.8, s32[24]{0:T(128)S(1)} %get-tuple-element.58, f32[24,128,256]{2,1,0:T(8,128)} %multiply_bitcast_fusion.6), kind=kCustom, calls=%fused_computation.25 | custom fusion | flops 786432 | bytes 9437280 | tf_op jit(solution)/shard_map/scatter-add | solution.py:65
  350.5 9.4 %scatter_fusion.10 = f32[48,128,256]{2,1,0:T(8,128)} fusion(f32[48,128,256]{2,1,0:T(8,128)} %scatter_fusion.9, s32[24]{0:T(128)S(1)} %get-tuple-element.59, f32[24,128,256]{2,1,0:T(8,128)} %multiply_bitcast_fusion.5), kind=kCustom, calls=%fused_computation.26 | custom fusion | flops 786432 | bytes 9437280 | tf_op jit(solution)/shard_map/scatter-add | solution.py:65
  359.9 9.4 %scatter_fusion.11 = f32[48,128,256]{2,1,0:T(8,128)} fusion(f32[48,128,256]{2,1,0:T(8,128)} %scatter_fusion.10, s32[24]{0:T(128)S(1)} %get-tuple-element.60, f32[24,128,256]{2,1,0:T(8,128)} %multiply_bitcast_fusion.4), kind=kCustom, calls=%fused_computation.27 | custom fusion | flops 786432 | bytes 9437280 | tf_op jit(solution)/shard_map/scatter-add | solution.py:65
  369.3 9.3 %scatter_fusion.12 = f32[48,128,256]{2,1,0:T(8,128)} fusion(f32[48,128,256]{2,1,0:T(8,128)} %scatter_fusion.11, s32[24]{0:T(128)S(1)} %get-tuple-element.61, f32[24,128,256]{2,1,0:T(8,128)} %multiply_bitcast_fusion.3), kind=kCustom, calls=%fused_computation.28 | custom fusion | flops 786432 | bytes 9437280 | tf_op jit(solution)/shard_map/scatter-add | solution.py:65
  378.7 9.5 %scatter_fusion.13 = f32[48,128,256]{2,1,0:T(8,128)} fusion(f32[48,128,256]{2,1,0:T(8,128)} %scatter_fusion.12, s32[24]{0:T(128)S(1)} %get-tuple-element.62, f32[24,128,256]{2,1,0:T(8,128)} %multiply_bitcast_fusion.2), kind=kCustom, calls=%fused_computation.29 | custom fusion | flops 786432 | bytes 9437280 | tf_op jit(solution)/shard_map/scatter-add | solution.py:65
  388.2 9.4 %scatter_fusion.14 = f32[48,128,256]{2,1,0:T(8,128)} fusion(f32[48,128,256]{2,1,0:T(8,128)} %scatter_fusion.13, s32[24]{0:T(128)S(1)} %get-tuple-element.63, f32[24,128,256]{2,1,0:T(8,128)} %multiply_bitcast_fusion.1), kind=kCustom, calls=%fused_computation.30 | custom fusion | flops 786432 | bytes 9437280 | tf_op jit(solution)/shard_map/scatter-add | solution.py:65
  411.0 74.2 %reduce-scatter.5.cloned.1.call-done = bf16[384,256]{1,0:T(8,128)(2,1)} async-done(((bf16[6144,256]{1,0:T(8,128)(2,1)}), bf16[384,256]{1,0:T(8,128)(2,1)}) %reduce-scatter.5.cloned.1.call-update) | async-done | bytes 196624 | tf_op jit(solution)/shard_map/reduce_scatter | solution.py:67
  487.2 14.3 %psum.30 = f32[256]{0:T(256)S(1)} all-reduce(f32[256]{0:T(256)S(1)} %get-tuple-element.13), channel_id=1, replica_groups=mesh['row'=16,'col'=8] {'col'}, use_global_device_ids=true, to_apply=%region_21.23 | all-reduce | flops 256 | bytes 2048 | tf_op jit(solution)/shard_map/psum | solution.py:8
  501.5 31.2 %psum.31 = f32[256]{0:T(256)S(1)} all-reduce(f32[256]{0:T(256)S(1)} %psum.30), channel_id=1, replica_groups=mesh['row'=16,'col'=8] {'row'}, use_global_device_ids=true, to_apply=%region_22.24 | all-reduce | flops 256 | bytes 2048 | tf_op jit(solution)/shard_map/psum | solution.py:9
  532.6 14.8 %all-reduce.3.cloned.1.call-done = f32[256,256]{0,1:T(8,128)} async-done(((f32[256,256]{0,1:T(8,128)}), f32[256,256]{0,1:T(8,128)}) %all-reduce.3.cloned.1.call-update) | async-done | bytes 262160 | tf_op jit(solution)/shard_map/psum | solution.py:8
  549.9 84.4 %all-reduce.5.cloned.1.call-done = f32[256,256]{0,1:T(8,128)} async-done(((f32[256,256]{0,1:T(8,128)}), f32[256,256]{0,1:T(8,128)}) %all-reduce.5.cloned.1.call-update) | async-done | bytes 262160 | tf_op jit(solution)/shard_map/psum | solution.py:9
  (138 shorter events, 150.7 us)
Async XLA Ops:
  7.2 53.3 %copy-start = (bf16[256,256]{1,0:T(8,128)(2,1)S(1)}, bf16[256,256]{1,0:T(8,128)(2,1)}, u32[]{:S(2)}) copy-start(bf16[256,256]{1,0:T(8,128)(2,1)} %param.10) | copy-start | bytes 393220
  7.2 53.2 %all-gather.3.cloned.1.call-start = ((), (), s32[]{:S(2)}) async-start(), calls=%async_computation.2 | async-start | bytes 3342336 | tf_op jit(solution)/shard_map/all_gather | solution.py:37
  7.9 11.9 %copy-start.18 = (s32[1,1,24,16]{2,3,1,0:T(8,128)S(1)}, s32[1,1,24,16]{2,3,1,0:T(8,128)}, u32[]{:S(2)}) copy-start(s32[1,1,24,16]{2,3,1,0:T(8,128)} %param.14) | copy-start | bytes 4612
  7.9 12.1 %copy-start.20 = (s32[1,1,24]{2,1,0:T(1,128)S(1)}, s32[1,1,24]{2,1,0:T(1,128)}, u32[]{:S(2)}) copy-start(s32[1,1,24]{2,1,0:T(1,128)} %param.15) | copy-start | bytes 292
  7.9 173.1 %reduce-scatter.3.cloned.1.call-start = ((), (), s32[]{:S(2)}) async-start(), calls=%async_computation.3 | async-start | bytes 1769472 | tf_op jit(solution)/shard_map/reduce_scatter | solution.py:44
  93.1 16.8 %slice-start = ((s8[12582912]{0:T(1024)(128)(4,1)}), s8[4194304]{0:T(1024)(128)(4,1)S(1)}, s32[]{:S(2)}) async-start(s8[12582912]{0:T(1024)(128)(4,1)} %bitcast.286), calls=%async_computation.8 | async-start | bytes 8388608
  95.5 3.6 copy-start.13
  95.6 14.4 %slice-start.1 = ((s8[12582912]{0:T(1024)(128)(4,1)}), s8[4194304]{0:T(1024)(128)(4,1)S(1)}, s32[]{:S(2)}) async-start(s8[12582912]{0:T(1024)(128)(4,1)} %bitcast.286), calls=%async_computation.9 | async-start | bytes 8388608
  99.2 3.6 copy-start.14
  102.7 3.6 copy-start.11
  102.7 7.2 %slice-start.2 = ((s8[12582912]{0:T(1024)(128)(4,1)}), s8[4194304]{0:T(1024)(128)(4,1)S(1)}, s32[]{:S(2)}) async-start(s8[12582912]{0:T(1024)(128)(4,1)} %bitcast.286), calls=%async_computation.10 | async-start | bytes 8388608
  106.4 3.6 copy-start.12
  128.7 2.5 copy-start.2
  133.4 47.6 %copy-start.17 = (bf16[384,256]{1,0:T(8,128)(2,1)S(1)}, bf16[384,256]{1,0:T(8,128)(2,1)}, u32[]{:S(2)}) copy-start(bf16[384,256]{1,0:T(8,128)(2,1)} %param.12) | copy-start | bytes 589828
  133.4 47.6 %copy-start.19 = (f32[256]{0:T(256)S(1)}, f32[256]{0:T(256)}, u32[]{:S(2)}) copy-start(f32[256]{0:T(256)} %param.11) | copy-start | bytes 3076
  151.2 58.8 %all-gather.5.cloned.1.call-start = ((), (), s32[]{:S(2)}) async-start(), calls=%async_computation.4 | async-start | bytes 1769472 | tf_op jit(solution)/shard_map/all_gather | solution.py:58
  183.0 302.3 %reduce-scatter.5.cloned.1.call-start = ((), (), s32[]{:S(2)}) async-start(), calls=%async_computation.5 | async-start | bytes 3342336 | tf_op jit(solution)/shard_map/reduce_scatter | solution.py:67
  210.1 4.2 copy-start.1
  210.1 18.3 %slice-start.3 = ((s8[12582912]{0:T(1024)(128)(4,1)}), s8[4194304]{0:T(1024)(128)(4,1)S(1)}, s32[]{:S(2)}) async-start(s8[12582912]{0:T(1024)(128)(4,1)} %bitcast.298), calls=%async_computation.11 | async-start | bytes 8388608
  214.2 14.1 %slice-start.4 = ((s8[12582912]{0:T(1024)(128)(4,1)}), s8[4194304]{0:T(1024)(128)(4,1)S(1)}, s32[]{:S(2)}) async-start(s8[12582912]{0:T(1024)(128)(4,1)} %bitcast.298), calls=%async_computation.12 | async-start | bytes 8388608
  221.2 7.1 %slice-start.5 = ((s8[12582912]{0:T(1024)(128)(4,1)}), s8[4194304]{0:T(1024)(128)(4,1)S(1)}, s32[]{:S(2)}) async-start(s8[12582912]{0:T(1024)(128)(4,1)} %bitcast.298), calls=%async_computation.13 | async-start | bytes 8388608
  410.9 74.3 %copy-start.16 = (bf16[384,256]{1,0:T(8,128)(2,1)S(1)}, bf16[384,256]{1,0:T(8,128)(2,1)}, u32[]{:S(2)}) copy-start(bf16[384,256]{1,0:T(8,128)(2,1)} %param.9) | copy-start | bytes 589828
  410.9 136.5 %all-reduce.3.cloned.1.call-start = ((), (), s32[]{:S(2)}) async-start(), calls=%async_computation.6 | async-start | bytes 524288 | tf_op jit(solution)/shard_map/psum | solution.py:8
  487.1 147.1 %all-reduce.5.cloned.1.call-start = ((), (), s32[]{:S(2)}) async-start(), calls=%async_computation.7 | async-start | bytes 524288 | tf_op jit(solution)/shard_map/psum | solution.py:9
  (9 other events, 21.3 us)
Sparse Core Ops, SparseCore 0:
  10.2 50.2 all-gather.2
  151.4 29.6 reduce-scatter.2
  183.3 26.6 all-gather.4
  411.1 74.1 reduce-scatter.4
  488.0 59.4 all-reduce.2
  550.5 83.7 all-reduce.4
